TPU v7x, 512 devices: a whole 4x8x8 slice. The times are simulated.
512 devices in a mesh: seq: 32 (over y, x), trow: 2 (over core), tcol: 8 (over z).
Axes of the slice: x: 4, y: 8, z: 8, core: 2. Of those that a mesh axis runs over, the one named last changes fastest.
Arguments:
- tokens: bfloat16 [16384, 4096], P('seq', ('trow', 'tcol')), may hold values from -24 to 24
- norm_gain: float32 [4096], replicated, may hold values from 0.1 to 1.9
- in_weight: bfloat16 [3, 4096, 8192], P(None, None, ('trow', 'tcol')), may hold values from -0.09375 to 0.09375
- filter_taps: float32 [128, 8192], P(None, ('trow', 'tcol')), may hold values from -0.5 to 0.5
- conv_skip: float32 [8192], P(('trow', 'tcol')), may hold values from -1 to 1
- out_weight: bfloat16 [8192, 4096], P(('trow', 'tcol')), may hold values from -0.09375 to 0.09375
Outputs:
- mixer_out: bfloat16 [16384, 4096], P('seq', ('trow', 'tcol'))
All inputs are finite; a program needn't handle non-finite values.
Results may differ from a plain program's by a relative error of at most 0.03.
Values may be sent and summed in bfloat16 or wider, within the bound.
A program may use at most 64 MiB of HBM per device.

v0:
```python
import jax
import jax.numpy as jnp
from jax import lax
from jax.sharding import PartitionSpec as P


def passed_along(block, axis, distance):
    devices = range(lax.axis_size(axis))
    route = [(i - distance, i) for i in devices if i - distance in devices]
    return lax.ppermute(block, axis, route)


def on_device(tokens, norm_gain, in_weight, filter_taps, conv_skip, out_weight):
    whole = lax.all_gather(tokens, ("trow", "tcol"), axis=1, tiled=True)
    wide = whole.astype(jnp.float32)
    mean_square = jnp.mean(wide * wide, axis=1, keepdims=True)
    normed = (wide * lax.rsqrt(mean_square + 1e-06) * norm_gain).astype(jnp.bfloat16)
    query = jnp.dot(normed, in_weight[0], preferred_element_type=jnp.float32).astype(jnp.bfloat16)
    keys = jnp.dot(normed, in_weight[1], preferred_element_type=jnp.float32).astype(jnp.bfloat16)
    values = jnp.dot(normed, in_weight[2], preferred_element_type=jnp.float32).astype(jnp.bfloat16)
    mixed = (keys.astype(jnp.float32) * values.astype(jnp.float32)).astype(jnp.bfloat16)
    taps = filter_taps.shape[0]
    rows = mixed.shape[0]
    channels = mixed.shape[1]
    tail_rows = mixed[rows - (taps - 1) :]
    previous = passed_along(tail_rows, "seq", 1)
    extended = jnp.concatenate([previous, mixed], axis=0)

    def tap_group(group, total):
        for inner in range(8):
            index = group * 8 + inner
            window = lax.dynamic_slice_in_dim(extended, taps - 1 - index, rows, 0)
            weight = lax.dynamic_slice_in_dim(filter_taps, index, 1, 0)
            total = total + window.astype(jnp.float32) * weight
        return total

    filtered = lax.fori_loop(0, taps // 8, tap_group, jnp.zeros((rows, channels), jnp.float32))
    filtered = filtered + conv_skip * mixed.astype(jnp.float32)
    gated = (query.astype(jnp.float32) * filtered).astype(jnp.bfloat16)
    partial_sum = jnp.dot(gated, out_weight, preferred_element_type=jnp.float32)
    summed = lax.psum_scatter(
        partial_sum.astype(jnp.bfloat16), ("trow", "tcol"), scatter_dimension=1, tiled=True
    )
    return summed


def solution(mesh):
    placed = (
        P("seq", ("trow", "tcol")),
        P(),
        P(None, None, ("trow", "tcol")),
        P(None, ("trow", "tcol")),
        P(("trow", "tcol")),
        P(("trow", "tcol"), None),
    )
    return jax.shard_map(
        on_device, mesh=mesh, in_specs=placed, out_specs=P("seq", ("trow", "tcol")), check_vma=False
    )
```

profile of v0, /device:TPU:1, one launch (start us, length us, event | category | flops | bytes accessed | tf_op | source)
XLA Modules:
  0.0 220.7 jit_solution(7478278523960679927)
XLA Ops:
  7.3 59.9 %all-gather.2.cloned.1.call-done = bf16[512,4096]{1,0:T(8,128)(2,1)} async-done(((bf16[512,256]{1,0:T(8,128)(2,1)}), bf16[512,4096]{1,0:T(8,128)(2,1)}) %all-gather.2.cloned.1.call-update) | async-done | bytes 4194320 | tf_op jit(solution)/shard_map/all_gather | solution.py:14
  67.2 3.2 %fusion.7 = f32[512]{0:T(512)S(1)} fusion(bf16[512,4096]{1,0:T(8,128)(2,1)} %all-gather.2.cloned.1.call-done), kind=kLoop, calls=%fused_computation.18 | loop fusion | flops 6290944 | bytes 4196352 | tf_op jit(solution)/shard_map/reduce_sum | solution.py:16
  70.6 4.6 %fusion.46 = f32[512,512]{1,0:T(8,128)S(1)} fusion(bf16[3,4096,512]{2,1,0:T(8,128)(2,1)} %param.10, bf16[512,4096]{1,0:T(8,128)(2,1)S(1)} %copy-done, f32[4096]{0:T(1024)S(1)} %copy-done.1, f32[512]{0:T(512)S(1)} %add_rsqrt_fusion), kind=kOutput, calls=%fused_computation.40 | convolution fusion | flops 2156396544 | bytes 9455616 | tf_op jit(solution)/shard_map/dot_general | solution.py:20
  75.2 4.6 %fusion.40 = bf16[512,512]{1,0:T(8,128)(2,1)S(1)} fusion(f32[512,512]{1,0:T(8,128)S(1)} %fusion.46, bf16[3,4096,512]{2,1,0:T(8,128)(2,1)} %param.10, bf16[512,4096]{1,0:T(8,128)(2,1)S(1)} %copy-done, f32[4096]{0:T(1024)S(1)} %copy-done.1, f32[512]{0:T(512)S(1)} %add_rsqrt_fusion), kind=kOutput, calls=%fused_computation.38 | convolution fusion | flops 2156920832 | bytes 9979904 | tf_op jit(solution)/shard_map/dot_general | solution.py:19
  79.8 3.1 %collective-permute-start = (bf16[127,512]{1,0:T(8,128)(2,1)S(1)}, bf16[127,512]{1,0:T(8,128)(2,1)S(1)}, u32[]{:S(2)}, u32[]{:S(2)}) collective-permute-start(bf16[127,512]{1,0:T(8,128)(2,1)S(1)} %slice.16), channel_id=1, source_target_pairs={{0,16},{16,32},{32,48},{48,64},{64,80},{80,96},{96,112},{112,128},... | collective-permute-start | bytes 390152 | tf_op jit(solution)/shard_map/ppermute | solution.py:10
  82.9 2.6 %collective-permute-done = bf16[127,512]{1,0:T(8,128)(2,1)S(1)} collective-permute-done((bf16[127,512]{1,0:T(8,128)(2,1)S(1)}, bf16[127,512]{1,0:T(8,128)(2,1)S(1)}, u32[]{:S(2)}, u32[]{:S(2)}) %collective-permute-start) | collective-permute-done | bytes 130080 | tf_op jit(solution)/shard_map/ppermute | solution.py:10
  85.6 39.9 %while.17 = (s32[]{:T(128)}, f32[512,512]{1,0:T(8,128)S(1)}, bf16[639,512]{1,0:T(8,128)(2,1)S(1)}, f32[128,512]{1,0:T(8,128)}, s32[]{:T(128)}, /*index=5*/s32[]{...) while((s32[]{:T(128)}, f32[512,512]{1,0:T(8,128)S(1)}, ...), condition=%wide.region_2.0_spmd.clone, body=%wide.region_1.0_spmd.clone.sunk | while | flops 6553667 | bytes 6341631 | solution.py:37
  86.8 1.4 fusion.58
  89.3 1.3 fusion.58
  91.8 1.4 fusion.58
  94.3 1.3 fusion.58
  96.8 1.4 fusion.58
  101.7 1.4 fusion.58
  104.2 1.3 fusion.58
  106.7 1.4 fusion.58
  109.2 1.3 fusion.58
  111.7 1.4 fusion.58
  114.2 1.3 fusion.58
  116.7 1.4 fusion.58
  119.2 1.3 fusion.58
  121.7 1.4 fusion.58
  124.2 1.3 fusion.58
  125.5 11.2 %convolution_convert_fusion = bf16[512,4096]{1,0:T(8,128)(2,1)} fusion(bf16[512,4096]{1,0:T(8,128)(2,1)} %param.13, bf16[3,4096,512]{2,1,0:T(8,128)(2,1)} %param.10, f32[512,512]{1,0:T(8,128)S(1)} %get-tuple-element.156, bf16[512,512]{1,0:T(8,128)(2,1)S(1)} %fusion.40, f32[512]{0:T(512)S(1)} %copy-done.2, ...), kind=kOutput, calls=%fused_computation.21 | convolution fusion | flops 4307288064 | bytes 18370560 | tf_op jit(solution)/shard_map/dot_general | solution.py:40
  136.8 77.0 %reduce-scatter.2.cloned.1.call-done = bf16[512,256]{1,0:T(8,128)(2,1)} async-done(((bf16[512,4096]{1,0:T(8,128)(2,1)}), bf16[512,256]{1,0:T(8,128)(2,1)}) %reduce-scatter.2.cloned.1.call-update) | async-done | bytes 262160 | tf_op jit(solution)/shard_map/reduce_scatter | solution.py:41
  (31 shorter events, 19.1 us)
Async XLA Ops:
  6.5 63.9 %copy-start.1 = (f32[4096]{0:T(1024)S(1)}, f32[4096]{0:T(1024)}, u32[]{:S(2)}) copy-start(f32[4096]{0:T(1024)} %param.9) | copy-start | bytes 49156
  6.5 60.6 %all-gather.2.cloned.1.call-start = ((), (), s32[]{:S(2)}) async-start(), calls=%async_computation.1 | async-start | bytes 4456448 | tf_op jit(solution)/shard_map/all_gather | solution.py:14
  7.3 206.6 %reduce-scatter.2.cloned.1.call-start = ((), (), s32[]{:S(2)}) async-start(), calls=%async_computation.2 | async-start | bytes 4456448 | tf_op jit(solution)/shard_map/reduce_scatter | solution.py:41
  67.2 3.4 %copy-start = (bf16[512,4096]{1,0:T(8,128)(2,1)S(1)}, bf16[512,4096]{1,0:T(8,128)(2,1)}, u32[]{:S(2)}) copy-start(bf16[512,4096]{1,0:T(8,128)(2,1)} %all-gather.2.cloned.1.call-done) | copy-start | bytes 12582916
  79.8 5.7 %collective-permute-start = (bf16[127,512]{1,0:T(8,128)(2,1)S(1)}, bf16[127,512]{1,0:T(8,128)(2,1)S(1)}, u32[]{:S(2)}, u32[]{:S(2)}) collective-permute-start(bf16[127,512]{1,0:T(8,128)(2,1)S(1)} %slice.16), channel_id=1, source_target_pairs={{0,16},{16,32},{32,48},{48,64},{64,80},{80,96},{96,112},{112,128},... | collective-permute-start | bytes 390152 | tf_op jit(solution)/shard_map/ppermute | solution.py:10
  85.6 39.9 %copy-start.2 = (f32[512]{0:T(512)S(1)}, f32[512]{0:T(512)}, u32[]{:S(2)}) copy-start(f32[512]{0:T(512)} %param.12) | copy-start | bytes 6148
Sparse Core Ops, SparseCore 0:
  9.4 57.7 all-gather.1
  136.9 76.8 reduce-scatter.1
where the time goes:
time: 222 us; the launch traced here: 221 us
  waiting for transfers between devices  140 us (63%)
  other arithmetic  25 us (11%)
  matrix products  20.4 us (9%)
  local copies, waits for them, and re-layouts  16.9 us (8%)
  between operations  13.5 us (6%)
  starting transfers between devices  3.13 us (1%)
    reduce_scatter x1, waiting for transfers between devices, on_device(): lax.psum_scatter(partial_sum.astype(jnp.bfloat16), ('trow', 'tcol'), scat...  77 us
    all_gather x1, waiting for transfers between devices, on_device(): whole = lax.all_gather(tokens, ('trow', 'tcol'), axis=1, tiled=True)  59.9 us
    add x16, other arithmetic, tap_group(): total = total + window.astype(jnp.float32) * weight  21.6 us
    dynamic_slice x16, local copies, waits for them, and re-layouts, tap_group(): weight = lax.dynamic_slice_in_dim(filter_taps, index, 1, 0)  16.6 us
    dot_general x1, matrix products, on_device(): partial_sum = jnp.dot(gated, out_weight, preferred_element_type=jnp.float32)  11.2 us
    dot_general x1, matrix products, on_device(): jnp.dot(normed, in_weight[1], preferred_element_type=jnp.float32)  4.58 us
    dot_general x1, matrix products, on_device(): jnp.dot(normed, in_weight[2], preferred_element_type=jnp.float32)  4.56 us
  transfers between devices with their start and end apart: 3, of which 3 were waited for; matrix products, arithmetic and copies ran while one was open for 0% of the time, Pallas kernels for 0%

commit v1 on v0

--- a/solution.py
+++ b/solution.py
@@ -11,7 +11,12 @@
 
 
 def on_device(tokens, norm_gain, in_weight, filter_taps, conv_skip, out_weight):
-    whole = lax.all_gather(tokens, ("trow", "tcol"), axis=1, tiled=True)
+    whole = jnp.concatenate(
+        lax.all_to_all(
+            jnp.stack([tokens] * lax.axis_size(("trow", "tcol"))), ("trow", "tcol"), 0, 0
+        ),
+        axis=1,
+    )
     wide = whole.astype(jnp.float32)
     mean_square = jnp.mean(wide * wide, axis=1, keepdims=True)
     normed = (wide * lax.rsqrt(mean_square + 1e-06) * norm_gain).astype(jnp.bfloat16)

time: 222 us -> 275 us (1.24)
  waiting for transfers between devices: 140 us -> 173 us
  starting transfers between devices: 3.13 us -> 15.1 us
  local copies, waits for them, and re-layouts: 16.9 us -> 20.2 us
    all_to_all x0 -> x1, waiting for transfers between devices: none -> 92.9 us  [on_device(): lax.all_to_all(jnp.stack([tokens] * lax.axis_size(('trow', 'tcol'))), ('t...]
    all_gather x1 -> x0, waiting for transfers between devices: 59.9 us -> none  [on_device(): whole = lax.all_gather(tokens, ('trow', 'tcol'), axis=1, tiled=True)]
    all_to_all x0 -> x1, starting transfers between devices: none -> 12 us  [on_device(): lax.all_to_all(jnp.stack([tokens] * lax.axis_size(('trow', 'tcol'))), ('t...]
    convert_element_type x0 -> x1, other arithmetic: none -> 2.77 us  [on_device(): (wide * lax.rsqrt(mean_square + 1e-06) * norm_gain).astype(jnp.bfloat16)]
where the time goes in v1:
time: 275 us; the launch traced here: 273 us
  waiting for transfers between devices  173 us (63%)
  other arithmetic  27.6 us (10%)
  matrix products  21.8 us (8%)
  local copies, waits for them, and re-layouts  20.2 us (7%)
  starting transfers between devices  15.1 us (5%)
  between operations  13.5 us (5%)
    all_to_all x1, waiting for transfers between devices, on_device(): lax.all_to_all(jnp.stack([tokens] * lax.axis_size(('trow', 'tcol'))), ('t...  92.9 us
    reduce_scatter x1, waiting for transfers between devices, on_device(): lax.psum_scatter(partial_sum.astype(jnp.bfloat16), ('trow', 'tcol'), scat...  77.6 us
    add x16, other arithmetic, tap_group(): total = total + window.astype(jnp.float32) * weight  21.6 us
    dynamic_slice x16, local copies, waits for them, and re-layouts, tap_group(): weight = lax.dynamic_slice_in_dim(filter_taps, index, 1, 0)  16.6 us
    all_to_all x1, starting transfers between devices, on_device(): lax.all_to_all(jnp.stack([tokens] * lax.axis_size(('trow', 'tcol'))), ('t...  12 us
    dot_general x1, matrix products, on_device(): partial_sum = jnp.dot(gated, out_weight, preferred_element_type=jnp.float32)  11.2 us
    dot_general x1, matrix products, on_device(): jnp.dot(normed, in_weight[2], preferred_element_type=jnp.float32)  6.05 us
  transfers between devices with their start and end apart: 3, of which 3 were waited for; matrix products, arithmetic and copies ran while one was open for 0% of the time, Pallas kernels for 0%

profile of v1, /device:TPU:1, one launch (start us, length us, event | category | flops | bytes accessed | tf_op | source)
XLA Modules:
  0.0 272.9 jit_solution(6088613121360569682)
XLA Ops:
  7.6 2.4 stack.2
  10.0 12.0 %all-to-all-start = ((bf16[16,512,256]{1,2,0:T(8,128)(2,1)}), bf16[16,512,256]{1,2,0:T(8,128)(2,1)}, u32[]{:S(2)}, u32[]{:S(2)}) async-start(bf16[16,512,256]{1,2,0:T(8,128)(2,1)} %stack.2), calls=%async_computation | async-start | bytes 8388608 | tf_op jit(solution)/shard_map/all_to_all | solution.py:15
  22.1 92.9 %all-to-all-done = bf16[16,512,256]{1,2,0:T(8,128)(2,1)} async-done(((bf16[16,512,256]{1,2,0:T(8,128)(2,1)}), bf16[16,512,256]{1,2,0:T(8,128)(2,1)}, u32[]{:S(2)}, u32[]{:S(2)}) %all-to-all-start) | async-done | bytes 4194336 | tf_op jit(solution)/shard_map/all_to_all | solution.py:15
  115.0 3.1 %fusion.7 = f32[512]{0:T(512)S(1)} fusion(bf16[16,512,256]{1,2,0:T(8,128)(2,1)} %all-to-all-done), kind=kLoop, calls=%fused_computation.18 | loop fusion | flops 6290944 | bytes 4196352 | tf_op jit(solution)/shard_map/reduce_sum | solution.py:21
  118.1 2.8 %fusion.9 = bf16[16,512,256]{1,2,0:T(8,128)(2,1)S(1)} fusion(bf16[16,512,256]{1,2,0:T(8,128)(2,1)} %all-to-all-done, f32[16,256]{1,0:T(8,128)S(1)} %mul.354, f32[512]{0:T(512)S(1)} %add_rsqrt_fusion), kind=kLoop, calls=%fused_computation.20 | loop fusion | flops 8388608 | bytes 8407040 | tf_op jit(solution)/shard_map/convert_element_type | solution.py:22
  120.9 6.1 %fusion.46 = f32[512,512]{1,0:T(8,128)S(1)} fusion(bf16[512,4096]{0,1:T(8,128)(2,1)S(1)} %bitcast.62, bf16[3,4096,512]{2,1,0:T(8,128)(2,1)} %param.10), kind=kOutput, calls=%fused_computation.40 | convolution fusion | flops 2148007936 | bytes 9437184 | tf_op jit(solution)/shard_map/dot_general | solution.py:25
  127.0 4.5 %fusion.40 = bf16[512,512]{1,0:T(8,128)(2,1)S(1)} fusion(f32[512,512]{1,0:T(8,128)S(1)} %fusion.46, bf16[512,4096]{0,1:T(8,128)(2,1)S(1)} %bitcast.63, bf16[3,4096,512]{2,1,0:T(8,128)(2,1)} %param.10), kind=kOutput, calls=%fused_computation.38 | convolution fusion | flops 2148532224 | bytes 9961472 | tf_op jit(solution)/shard_map/dot_general | solution.py:24
  131.6 3.1 %collective-permute-start = (bf16[127,512]{1,0:T(8,128)(2,1)S(1)}, bf16[127,512]{1,0:T(8,128)(2,1)S(1)}, u32[]{:S(2)}, u32[]{:S(2)}) collective-permute-start(bf16[127,512]{1,0:T(8,128)(2,1)S(1)} %slice.16), channel_id=1, source_target_pairs={{0,16},{16,32},{32,48},{48,64},{64,80},{80,96},{96,112},{112,128},... | collective-permute-start | bytes 390152 | tf_op jit(solution)/shard_map/ppermute | solution.py:10
  134.7 2.5 collective-permute-done
  137.4 39.9 %while.17 = (s32[]{:T(128)}, f32[512,512]{1,0:T(8,128)S(1)}, bf16[639,512]{1,0:T(8,128)(2,1)S(1)}, f32[128,512]{1,0:T(8,128)}, s32[]{:T(128)}, /*index=5*/s32[]{...) while((s32[]{:T(128)}, f32[512,512]{1,0:T(8,128)S(1)}, ...), condition=%wide.region_2.0_spmd.clone, body=%wide.region_1.0_spmd.clone.sunk | while | flops 6553667 | bytes 6341631 | solution.py:42
  138.5 1.4 fusion.57
  143.5 1.4 fusion.57
  146.0 1.3 fusion.57
  148.5 1.4 fusion.57
  151.0 1.3 fusion.57
  153.5 1.4 fusion.57
  158.4 1.4 fusion.57
  163.4 1.4 fusion.57
  165.9 1.3 fusion.57
  168.4 1.4 fusion.57
  170.9 1.3 fusion.57
  173.4 1.4 fusion.57
  177.3 11.2 %convolution_convert_fusion = bf16[512,4096]{1,0:T(8,128)(2,1)} fusion(bf16[512,4096]{1,0:T(8,128)(2,1)} %param.13, bf16[512,4096]{0,1:T(8,128)(2,1)} %bitcast.64, bf16[3,4096,512]{2,1,0:T(8,128)(2,1)} %param.10, f32[512,512]{1,0:T(8,128)S(1)} %get-tuple-element.156, bf16[512,512]{1,0:T(8,128)(2,1)S(1)} %fusion.40, f32[512]{0:T(512)S(1)} %copy-done.2), kind=kOutput, calls=%fused_computation.21 | convolution fusion | flops 4298899456 | bytes 18352128 | tf_op jit(solution)/shard_map/dot_general | solution.py:45
  188.5 77.6 %reduce-scatter.2.cloned.1.call-done = bf16[512,256]{1,0:T(8,128)(2,1)} async-done(((bf16[512,4096]{1,0:T(8,128)(2,1)}), bf16[512,256]{1,0:T(8,128)(2,1)}) %reduce-scatter.2.cloned.1.call-update) | async-done | bytes 262160 | tf_op jit(solution)/shard_map/reduce_scatter | solution.py:46
  (34 shorter events, 23.4 us)
Async XLA Ops:
  10.0 12.0 %copy-start.1 = (f32[4096]{0:T(1024)S(1)}, f32[4096]{0:T(1024)}, u32[]{:S(2)}) copy-start(f32[4096]{0:T(1024)} %param.9) | copy-start | bytes 49156
  10.0 104.9 %all-to-all-start = ((bf16[16,512,256]{1,2,0:T(8,128)(2,1)}), bf16[16,512,256]{1,2,0:T(8,128)(2,1)}, u32[]{:S(2)}, u32[]{:S(2)}) async-start(bf16[16,512,256]{1,2,0:T(8,128)(2,1)} %stack.2), calls=%async_computation | async-start | bytes 8388608 | tf_op jit(solution)/shard_map/all_to_all | solution.py:15
  22.0 244.1 %reduce-scatter.2.cloned.1.call-start = ((), (), s32[]{:S(2)}) async-start(), calls=%async_computation.2 | async-start | bytes 4456448 | tf_op jit(solution)/shard_map/reduce_scatter | solution.py:46
  120.9 6.1 %copy-start = (bf16[16,512,256]{1,2,0:T(8,128)(2,1)}, bf16[16,512,256]{1,2,0:T(8,128)(2,1)S(1)}, u32[]{:S(2)}) copy-start(bf16[16,512,256]{1,2,0:T(8,128)(2,1)S(1)} %fusion.9) | copy-start | bytes 12582916
  131.6 5.7 %collective-permute-start = (bf16[127,512]{1,0:T(8,128)(2,1)S(1)}, bf16[127,512]{1,0:T(8,128)(2,1)S(1)}, u32[]{:S(2)}, u32[]{:S(2)}) collective-permute-start(bf16[127,512]{1,0:T(8,128)(2,1)S(1)} %slice.16), channel_id=1, source_target_pairs={{0,16},{16,32},{32,48},{48,64},{64,80},{80,96},{96,112},{112,128},... | collective-permute-start | bytes 390152 | tf_op jit(solution)/shard_map/ppermute | solution.py:10
  137.3 39.9 %copy-start.2 = (f32[512]{0:T(512)S(1)}, f32[512]{0:T(512)}, u32[]{:S(2)}) copy-start(f32[512]{0:T(512)} %param.12) | copy-start | bytes 6148
Sparse Core Ops, SparseCore 0:
  188.6 77.4 reduce-scatter.1
